TPU v7x, 256 devices: a whole 4x4x8 slice. The times are simulated.
256 devices in a mesh: store: 8 (over y, core), tensor: 32 (over z, x).
Axes of the slice: x: 4, y: 4, z: 8, core: 2. Of those that a mesh axis runs over, the one named last changes fastest.
Arguments:
- decoder_rows: bfloat16 [16384, 4096], P(('store', 'tensor')), may hold values from -45 to 45
- q_weight: bfloat16 [4096, 4096], P(None, 'tensor'), may hold values from -0.09375 to 0.09375
- kv_weight: bfloat16 [2, 896, 4096], P(None, None, 'tensor'), may hold values from -0.1875 to 0.1875
- out_weight: bfloat16 [4096, 4096], P('tensor'), may hold values from -0.5 to 0.5
- store_tiles: bfloat16 [4096, 128, 896], P('store', 'tensor'), may hold values from -6 to 6
- neighbour_shard: int32 [256, 2], replicated, may hold values from 0 to 7, all different within a row; in each aligned block of 32 rows (0 to 31, 32 to 63, ...) at most 12 rows name the same one
- neighbour_tile: int32 [256, 2], replicated, may hold values from 0 to 511
Outputs:
- cross: bfloat16 [16384, 4096], P(('store', 'tensor'))
Inputs may be any that keep to these rules, and one draw needn't show every extreme that they name: `neighbour_shard`: each block's 2 neighbours lie in different shards; among the 32 blocks of one sequence no shard is named more than 12 times, and in some sequence one shard is named exactly 12 times.
All inputs are finite; a program needn't handle non-finite values.
Results may differ from a plain program's by a relative error of at most 0.023.
Values may be sent and summed in bfloat16 or wider, within the bound.
No kernel may reach another device: no remote copies, remote signals or barrier semaphores. Data moves between devices by JAX's collectives and lax.ppermute only.
A program may use at most 128 MiB of HBM per device.

v0:
```python
import math
import jax
import jax.numpy as jnp
from jax import lax
from jax.sharding import PartitionSpec as P

HD = 128
BLOCK = 64
NTOK = 128
NEIGH = 2


def body(
    decoder_rows, q_weight, kv_weight, out_weight, store_tiles, neighbour_shard, neighbour_tile
):
    tensor_count = lax.axis_size("tensor")
    store_count = lax.axis_size("store")
    my_sequence = lax.axis_index("store")
    local_rows = decoder_rows.shape[0]
    seq_len = local_rows * tensor_count
    block_count = seq_len // BLOCK
    request_count = block_count * NEIGH
    capacity = 3 * request_count // (2 * store_count)
    head_cols = q_weight.shape[1]
    head_count = head_cols // HD
    q_factor = 1.0 / math.sqrt(HD)
    rows_wide = decoder_rows.astype(jnp.float32)
    normed = (
        rows_wide * lax.rsqrt(jnp.mean(rows_wide * rows_wide, axis=1, keepdims=True) + 1e-05)
    ).astype(jnp.bfloat16)
    queries = (
        jnp.dot(
            lax.all_gather(normed, "tensor", axis=0, tiled=True),
            q_weight,
            preferred_element_type=jnp.float32,
        )
        * q_factor
    ).astype(jnp.bfloat16)
    shard_table = neighbour_shard.reshape(store_count, request_count)
    tile_table = neighbour_tile.reshape(store_count, request_count)
    positions = jnp.arange(request_count, dtype=jnp.int32)
    before_mask = positions[None, :] < positions[:, None]
    same_shard = shard_table[:, :, None] == shard_table[:, None, :]
    rank_table = jnp.sum((same_shard & before_mask[None]).astype(jnp.int32), axis=2)
    served_here = shard_table == my_sequence
    slot_ids = jnp.arange(capacity, dtype=jnp.int32)
    slot_match = (
        served_here[:, :, None] & (rank_table[:, :, None] == slot_ids[None, None, :])
    ).astype(jnp.int32)
    slot_tile = jnp.sum(slot_match * tile_table[:, :, None], axis=1)
    outgoing = jnp.take(store_tiles, slot_tile.reshape(-1), axis=0)
    arrived = lax.all_to_all(outgoing, "store", split_axis=0, concat_axis=0, tiled=True)
    own_shard = lax.dynamic_index_in_dim(shard_table, my_sequence, 0, keepdims=False)
    own_rank = lax.dynamic_index_in_dim(rank_table, my_sequence, 0, keepdims=False)
    slot_index = own_shard * capacity + own_rank
    projected = jnp.einsum(
        "rne,ced->rncd",
        jnp.take(lax.all_gather(arrived, "tensor", axis=1, tiled=True), slot_index, axis=0),
        kv_weight,
        preferred_element_type=jnp.float32,
    )
    keys_values = projected.astype(jnp.bfloat16)
    keyed = keys_values.reshape(block_count, NEIGH * NTOK, 2, head_count, HD)
    query_blocks = queries.reshape(block_count, BLOCK, head_count, HD)
    scores = jnp.einsum(
        "cqhd,ckhd->chqk", query_blocks, keyed[:, :, 0], preferred_element_type=jnp.float32
    )
    expo_scores = jnp.exp(scores)
    weights = (expo_scores / jnp.sum(expo_scores, axis=3, keepdims=True)).astype(jnp.bfloat16)
    attended = jnp.einsum(
        "chqk,ckhd->cqhd", weights, keyed[:, :, 1], preferred_element_type=jnp.float32
    )
    attended = attended.astype(jnp.bfloat16).reshape(seq_len, head_cols)
    return lax.psum_scatter(
        jnp.dot(attended, out_weight, preferred_element_type=jnp.float32).astype(jnp.bfloat16),
        "tensor",
        scatter_dimension=0,
        tiled=True,
    )


def solution(mesh):
    in_specs = (
        P(("store", "tensor"), None),
        P(None, "tensor"),
        P(None, None, "tensor"),
        P("tensor", None),
        P("store", "tensor", None),
        P(),
        P(),
    )
    out_specs = P(("store", "tensor"), None)
    return jax.shard_map(body, mesh=mesh, in_specs=in_specs, out_specs=out_specs, check_vma=False)
```

profile of v0, /device:TPU:16, one launch (start us, length us, event | category | flops | bytes accessed | tf_op | source)
XLA Modules:
  0.0 625.0 jit_solution(14406171586889492786)
XLA Ops:
  6.5 1.4 fusion.12
  8.0 2.0 fusion.13
  10.0 0.8 copy.26
  10.8 0.1 reshape.146
  11.0 0.8 copy.27
  11.8 0.1 mul.46
  11.9 0.3 convert_reduce_fusion
  12.3 0.3 select_reduce_fusion
  12.8 3.2 gather_fusion
  16.1 0.4 broadcast_select_fusion
  16.5 14.0 %all_to_all.5 = bf16[96,4,896]{2,1,0:T(4,128)(2,1)S(1)} all-to-all(bf16[96,4,896]{2,1,0:T(4,128)(2,1)S(1)} %broadcast_select_fusion), channel_id=1, replica_groups=mesh['store'=8,'tensor'=32] {'store'}, dimensions={0} | all-to-all | bytes 1376256 | tf_op jit(solution)/shard_map/all_to_all | solution.py:52
  30.4 0.9 copy.30
  31.4 0.2 reduce-scatter.2.cloned.1.call-start
  31.7 121.8 %all-gather.5.cloned.1.call-done = bf16[2048,4096]{1,0:T(8,128)(2,1)} async-done(((bf16[64,4096]{1,0:T(8,128)(2,1)}), bf16[2048,4096]{1,0:T(8,128)(2,1)}) %all-gather.5.cloned.1.call-update) | async-done | bytes 16777232 | tf_op jit(solution)/shard_map/all_gather | solution.py:33
  153.5 8.2 %fusion.8 = bf16[2048,128]{1,0:T(8,128)(2,1)S(1)} fusion(bf16[2048,4096]{1,0:T(8,128)(2,1)} %all-gather.5.cloned.1.call-done, bf16[4096,128]{1,0:T(8,128)(2,1)S(1)} %copy-done.1), kind=kOutput, calls=%fused_computation.10 | convolution fusion | flops 2148007936 | bytes 18350080 | tf_op jit(solution)/shard_map/dot_general | solution.py:32
  161.7 158.3 %all-gather.3.cloned.1.call-done = bf16[96,128,896]{2,0,1:T(8,128)(2,1)} async-done(((bf16[96,4,896]{2,0,1:T(8,128)(2,1)}), bf16[96,128,896]{2,0,1:T(8,128)(2,1)}) %all-gather.3.cloned.1.call-update) | async-done | bytes 22020112 | tf_op jit(solution)/shard_map/all_gather | solution.py:58
  320.0 21.1 %copy.31 = bf16[96,128,896]{2,1,0:T(8,128)(2,1)} copy(bf16[96,128,896]{2,0,1:T(8,128)(2,1)} %all-gather.3.cloned.1.call-done) | data formatting | bytes 44040192 | tf_op jit(solution)/shard_map/all_gather | solution.py:58
  341.1 15.7 %gather_fusion.1 = bf16[64,128,896]{2,1,0:T(8,128)(2,1)} fusion(bf16[96,128,896]{2,1,0:T(8,128)(2,1)} %copy.31, s32[1024]{0:T(1024)S(1)} %pad_clamp_fusion), kind=kCustom, calls=%fused_computation.1 | custom fusion | bytes 29360384 | tf_op jit(solution)/shard_map/jit(_take)/gather | solution.py:58
  356.8 9.8 %fusion.5 = bf16[64,128,2,128]{3,1,2,0:T(8,128)(2,1)S(1)} fusion(bf16[64,128,896]{2,1,0:T(8,128)(2,1)} %gather_fusion.1, pred[64]{0:T(512)(128)(4,1)S(1)} %get-tuple-element.5, bf16[2,896,128]{2,1,0:T(8,128)(2,1)S(1)} %copy-done.2), kind=kOutput, calls=%fused_computation.8 | convolution fusion | flops 3767533568 | bytes 19333184 | tf_op jit(solution)/shard_map/rne,ced->rncd/dot_general | solution.py:56
  366.6 0.3 copy.32
  366.9 0.9 exponential_reduce_fusion
  367.8 0.6 fusion.11
  368.5 8.3 %convolution_convert_fusion = bf16[2048,4096]{1,0:T(8,128)(2,1)} fusion(bf16[2048,128]{1,0:T(8,128)(2,1)S(1)} %bitcast.45, bf16[128,4096]{1,0:T(8,128)(2,1)S(1)} %copy-done), kind=kOutput, calls=%fused_computation.2 | convolution fusion | flops 2155872256 | bytes 18350080 | tf_op jit(solution)/shard_map/dot_general | solution.py:75
  376.8 241.7 %reduce-scatter.2.cloned.1.call-done = bf16[64,4096]{1,0:T(8,128)(2,1)} async-done(((bf16[2048,4096]{1,0:T(8,128)(2,1)}), bf16[64,4096]{1,0:T(8,128)(2,1)}) %reduce-scatter.2.cloned.1.call-update) | async-done | bytes 524304 | tf_op jit(solution)/shard_map/reduce_scatter | solution.py:74
  (23 shorter events, 0.4 us)
Async XLA Ops:
  6.5 361.9 %copy-start = (bf16[128,4096]{1,0:T(8,128)(2,1)S(1)}, bf16[128,4096]{1,0:T(8,128)(2,1)}, u32[]{:S(2)}) copy-start(bf16[128,4096]{1,0:T(8,128)(2,1)} %param.10) | copy-start | bytes 3145732
  6.5 146.9 %copy-start.1 = (bf16[4096,128]{1,0:T(8,128)(2,1)S(1)}, bf16[4096,128]{1,0:T(8,128)(2,1)}, u32[]{:S(2)}) copy-start(bf16[4096,128]{1,0:T(8,128)(2,1)} %param.8) | copy-start | bytes 3145732
  6.5 146.9 %all-gather.5.cloned.1.call-start = ((), (), s32[]{:S(2)}) async-start(), calls=%async_computation.3 | async-start | bytes 17301504 | tf_op jit(solution)/shard_map/all_gather | solution.py:33
  10.0 310.0 %all-gather.3.cloned.1.call-start = ((), (), s32[]{:S(2)}) async-start(), calls=%async_computation.2 | async-start | bytes 22708224 | tf_op jit(solution)/shard_map/all_gather | solution.py:58
  31.4 587.1 %reduce-scatter.2.cloned.1.call-start = ((), (), s32[]{:S(2)}) async-start(), calls=%async_computation.4 | async-start | bytes 17301504 | tf_op jit(solution)/shard_map/reduce_scatter | solution.py:74
  341.1 15.7 %copy-start.2 = (bf16[2,896,128]{2,1,0:T(8,128)(2,1)S(1)}, bf16[2,896,128]{2,1,0:T(8,128)(2,1)}, u32[]{:S(2)}) copy-start(bf16[2,896,128]{2,1,0:T(8,128)(2,1)} %param.9) | copy-start | bytes 1376260
Sparse Core Ops, SparseCore 0:
  10.1 143.3 all-gather.4
  156.0 163.8 all-gather.2
  376.9 241.5 reduce-scatter.1
where the time goes:
time: 625 us
  waiting for transfers between devices  522 us (84%)
  local copies, waits for them, and re-layouts  43.4 us (7%)
  matrix products  27.8 us (4%)
  blocking collectives  14 us (2%)
  between operations  13.3 us (2%)
    reduce_scatter x1, waiting for transfers between devices, body(): lax.psum_scatter(jnp.dot(attended, out_weight, preferred_element_type=jnp...  242 us
    all_gather x1, waiting for transfers between devices, body(): lax.all_gather(arrived, 'tensor', axis=1, tiled=True)  158 us
    all_gather x1, waiting for transfers between devices, body(): lax.all_gather(normed, 'tensor', axis=0, tiled=True)  122 us
    all_gather x1, local copies, waits for them, and re-layouts, body(): lax.all_gather(arrived, 'tensor', axis=1, tiled=True)  21.1 us
    gather x1, local copies, waits for them, and re-layouts, body(): jnp.take(lax.all_gather(arrived, 'tensor', axis=1, tiled=True), slot_inde...  15.7 us
    all_to_all x1, blocking collectives, body(): lax.all_to_all(outgoing, 'store', split_axis=0, concat_axis=0, tiled=True)  14 us
  transfers between devices with their start and end apart: 3, of which 3 were waited for; matrix products, arithmetic and copies ran while one was open for 2% of the time, Pallas kernels for 0%

commit v1 on v0

--- a/solution.py
+++ b/solution.py
@@ -55,7 +55,14 @@
     slot_index = own_shard * capacity + own_rank
     projected = jnp.einsum(
         "rne,ced->rncd",
-        jnp.take(lax.all_gather(arrived, "tensor", axis=1, tiled=True), slot_index, axis=0),
+        jnp.take(
+            jnp.concatenate(
+                lax.all_to_all(jnp.stack([arrived] * lax.axis_size("tensor")), "tensor", 0, 0),
+                axis=1,
+            ),
+            slot_index,
+            axis=0,
+        ),
         kv_weight,
         preferred_element_type=jnp.float32,
     )

time: 625 us -> 971 us (1.55)
  waiting for transfers between devices: 522 us -> 850 us
  starting transfers between devices: 0.27 us -> 11.8 us
    all_gather x1, waiting for transfers between devices: 122 us -> 407 us  [body(): lax.all_gather(normed, 'tensor', axis=0, tiled=True)]
    all_to_all x0 -> x1, waiting for transfers between devices: none -> 180 us  [body(): lax.all_to_all(jnp.stack([arrived] * lax.axis_size('tensor')), 'tensor',...]
    all_gather x1 -> x0, waiting for transfers between devices: 158 us -> none  [body(): lax.all_gather(arrived, 'tensor', axis=1, tiled=True)]
    reduce_scatter x1, waiting for transfers between devices: 242 us -> 263 us  [body(): lax.psum_scatter(jnp.dot(attended, out_weight, preferred_element_type=jnp...]
    reshape x0 -> x1, local copies, waits for them, and re-layouts: none -> 21.1 us  [body(): jnp.concatenate(lax.all_to_all(jnp.stack([arrived] * lax.axis_size('tenso...]
    all_gather x1 -> x0, local copies, waits for them, and re-layouts: 21.1 us -> none  [body(): lax.all_gather(arrived, 'tensor', axis=1, tiled=True)]
    all_to_all x0 -> x1, starting transfers between devices: none -> 11.6 us  [body(): lax.all_to_all(jnp.stack([arrived] * lax.axis_size('tensor')), 'tensor',...]
  transfers between devices with their start and end apart: 3 -> 3, of which waited for: 3 -> 3; matrix products, arithmetic and copies ran while one was open for 2% -> 1% of each run, Pallas kernels for 0% -> 0%
where the time goes in v1:
time: 971 us
  waiting for transfers between devices  850 us (88%)
  local copies, waits for them, and re-layouts  51.5 us (5%)
  matrix products  27.8 us (3%)
  blocking collectives  14 us (1%)
  between operations  13.6 us (1%)
  starting transfers between devices  11.8 us (1%)
    all_gather x1, waiting for transfers between devices, body(): lax.all_gather(normed, 'tensor', axis=0, tiled=True)  407 us
    reduce_scatter x1, waiting for transfers between devices, body(): lax.psum_scatter(jnp.dot(attended, out_weight, preferred_element_type=jnp...  263 us
    all_to_all x1, waiting for transfers between devices, body(): lax.all_to_all(jnp.stack([arrived] * lax.axis_size('tensor')), 'tensor',...  180 us
    reshape x1, local copies, waits for them, and re-layouts, body(): jnp.concatenate(lax.all_to_all(jnp.stack([arrived] * lax.axis_size('tenso...  21.1 us
  transfers between devices with their start and end apart: 3, of which 3 were waited for; matrix products, arithmetic and copies ran while one was open for 1% of the time, Pallas kernels for 0%

profile of v1, /device:TPU:16, one launch (start us, length us, event | category | flops | bytes accessed | tf_op | source)
XLA Modules:
  0.0 970.5 jit_solution(7705670971197079789)
XLA Ops:
  6.6 0.9 copy.22
  7.6 0.3 convert_reduce_fusion
  7.9 0.8 copy.23
  8.7 0.1 mul.46
  8.9 0.3 select_reduce_fusion
  9.4 3.2 gather_fusion
  12.7 0.4 broadcast_select_fusion
  13.1 14.0 %all_to_all.10 = bf16[96,4,896]{2,1,0:T(4,128)(2,1)S(1)} all-to-all(bf16[96,4,896]{2,1,0:T(4,128)(2,1)S(1)} %broadcast_select_fusion), channel_id=1, replica_groups=mesh['store'=8,'tensor'=32] {'store'}, dimensions={0} | all-to-all | bytes 1376256 | tf_op jit(solution)/shard_map/all_to_all | solution.py:52
  27.1 8.8 stack.2
  35.9 11.6 %all-to-all-start.1 = ((bf16[32,96,4,896]{3,1,2,0:T(8,128)(2,1)}), bf16[32,96,4,896]{3,1,2,0:T(8,128)(2,1)}, u32[]{:S(2)}, u32[]{:S(2)}) async-start(bf16[32,96,4,896]{3,1,2,0:T(8,128)(2,1)} %stack.2), calls=%async_computation.1 | async-start | bytes 44040192 | tf_op jit(solution)/shard_map/all_to_all | solution.py:60
  47.6 0.2 fusion.12
  47.8 1.0 fusion.13
  48.8 0.2 reduce-scatter.2.cloned.1.call-start
  49.1 406.5 %all-gather.2.cloned.1.call-done = bf16[2048,4096]{1,0:T(8,128)(2,1)} async-done(((bf16[64,4096]{1,0:T(8,128)(2,1)}), bf16[2048,4096]{1,0:T(8,128)(2,1)}) %all-gather.2.cloned.1.call-update) | async-done | bytes 16777232 | tf_op jit(solution)/shard_map/all_gather | solution.py:33
  455.6 8.2 fusion.8
  463.8 180.1 %all-to-all-done.1 = bf16[32,96,4,896]{3,1,2,0:T(8,128)(2,1)} async-done(((bf16[32,96,4,896]{3,1,2,0:T(8,128)(2,1)}), bf16[32,96,4,896]{3,1,2,0:T(8,128)(2,1)}, u32[]{:S(2)}, u32[]{:S(2)}) %all-to-all-start.1) | async-done | bytes 22020128 | tf_op jit(solution)/shard_map/all_to_all | solution.py:60
  643.9 21.1 %copy.27 = bf16[96,128,896]{2,1,0:T(8,128)(2,1)} copy(bf16[96,128,896]{2,0,1:T(8,128)(2,1)} %bitcast.3) | data formatting | bytes 44040192 | tf_op jit(solution)/shard_map/reshape | solution.py:59
  665.1 15.7 %gather_fusion.1 = bf16[64,128,896]{2,1,0:T(8,128)(2,1)} fusion(bf16[96,128,896]{2,1,0:T(8,128)(2,1)} %copy.27, s32[1024]{0:T(1024)S(1)} %pad_clamp_fusion), kind=kCustom, calls=%fused_computation.1 | custom fusion | bytes 29360384 | tf_op jit(solution)/shard_map/jit(_take)/gather | solution.py:58
  680.8 9.8 %fusion.5 = bf16[64,128,2,128]{3,1,2,0:T(8,128)(2,1)S(1)} fusion(bf16[64,128,896]{2,1,0:T(8,128)(2,1)} %gather_fusion.1, pred[64]{0:T(512)(128)(4,1)S(1)} %get-tuple-element.5, bf16[2,896,128]{2,1,0:T(8,128)(2,1)S(1)} %copy-done.3), kind=kOutput, calls=%fused_computation.8 | convolution fusion | flops 3767533568 | bytes 19333184 | tf_op jit(solution)/shard_map/rne,ced->rncd/dot_general | solution.py:56
  690.5 0.3 copy.28
  690.8 0.9 exponential_reduce_fusion
  691.8 0.6 fusion.11
  692.4 8.3 convolution_convert_fusion
  700.7 262.9 %reduce-scatter.2.cloned.1.call-done = bf16[64,4096]{1,0:T(8,128)(2,1)} async-done(((bf16[2048,4096]{1,0:T(8,128)(2,1)}), bf16[64,4096]{1,0:T(8,128)(2,1)}) %reduce-scatter.2.cloned.1.call-update) | async-done | bytes 524304 | tf_op jit(solution)/shard_map/reduce_scatter | solution.py:81
  (25 shorter events, 0.6 us)
Async XLA Ops:
  6.5 685.9 %copy-start = (bf16[128,4096]{1,0:T(8,128)(2,1)S(1)}, bf16[128,4096]{1,0:T(8,128)(2,1)}, u32[]{:S(2)}) copy-start(bf16[128,4096]{1,0:T(8,128)(2,1)} %param.10) | copy-start | bytes 3145732
  35.9 11.6 %copy-start.1 = (bf16[64,4096]{1,0:T(8,128)(2,1)S(1)}, bf16[64,4096]{1,0:T(8,128)(2,1)}, u32[]{:S(2)}) copy-start(bf16[64,4096]{1,0:T(8,128)(2,1)} %param.7) | copy-start | bytes 1572868
  35.9 419.7 %copy-start.2 = (bf16[4096,128]{1,0:T(8,128)(2,1)S(1)}, bf16[4096,128]{1,0:T(8,128)(2,1)}, u32[]{:S(2)}) copy-start(bf16[4096,128]{1,0:T(8,128)(2,1)} %param.8) | copy-start | bytes 3145732
  35.9 608.0 %all-to-all-start.1 = ((bf16[32,96,4,896]{3,1,2,0:T(8,128)(2,1)}), bf16[32,96,4,896]{3,1,2,0:T(8,128)(2,1)}, u32[]{:S(2)}, u32[]{:S(2)}) async-start(bf16[32,96,4,896]{3,1,2,0:T(8,128)(2,1)} %stack.2), calls=%async_computation.1 | async-start | bytes 44040192 | tf_op jit(solution)/shard_map/all_to_all | solution.py:60
  47.5 408.1 %all-gather.2.cloned.1.call-start = ((), (), s32[]{:S(2)}) async-start(), calls=%async_computation.3 | async-start | bytes 17301504 | tf_op jit(solution)/shard_map/all_gather | solution.py:33
  48.8 914.9 %reduce-scatter.2.cloned.1.call-start = ((), (), s32[]{:S(2)}) async-start(), calls=%async_computation.4 | async-start | bytes 17301504 | tf_op jit(solution)/shard_map/reduce_scatter | solution.py:81
  665.1 15.7 %copy-start.3 = (bf16[2,896,128]{2,1,0:T(8,128)(2,1)S(1)}, bf16[2,896,128]{2,1,0:T(8,128)(2,1)}, u32[]{:S(2)}) copy-start(bf16[2,896,128]{2,1,0:T(8,128)(2,1)} %param.9) | copy-start | bytes 1376260
Sparse Core Ops, SparseCore 0:
  50.9 404.6 all-gather.1
  700.8 262.7 reduce-scatter.1
